TPU v7x, 32 devices: a whole 2x2x4 slice. The times are simulated.
32 devices in a mesh: parts: 2 (over x), node: 4 (over z), local: 4 (over y, core).
Axes of the slice: x: 2, y: 2, z: 4, core: 2. Of those that a mesh axis runs over, the one named last changes fastest.
Arguments:
- tokens: bfloat16 [256, 7168], P(('parts', 'node', 'local')), parts along dimension 0, may hold values from -6 to 6
- expert_ids: int32 [256, 8], P(('parts', 'node', 'local')), parts along dimension 0, may hold values from 0 to 7, as said below
- gate_weights: bfloat16 [256, 8], P(('parts', 'node', 'local')), parts along dimension 0, may hold values from 0.099609375 to 1
- slots: int32 [256, 4], P(('parts', 'node', 'local')), parts along dimension 0, may hold values from 0 to 8, as said below
- w_gate: bfloat16 [16, 7168, 2048], P(('parts', 'node'), None, 'local'), parts along dimension 0, may hold values from -0.0625 to 0.0625
- w_up: bfloat16 [16, 7168, 2048], P(('parts', 'node'), None, 'local'), parts along dimension 0, may hold values from -0.0625 to 0.0625
- w_down: bfloat16 [16, 2048, 7168], P(('parts', 'node'), 'local'), parts along dimension 0, may hold values from -0.125 to 0.125
Outputs:
- combined: bfloat16 [256, 7168], P(('parts', 'node', 'local')), parts along dimension 0
There are 2 independent parts, one for each index of `parts`. A program takes and returns all parts, laid end to end along the dimension named above; each array names one. Nothing has to cross between parts.
Inputs may be any that keep to these rules, and one draw needn't show every extreme that they name: `expert_ids`: each row names 8 different experts, all within at most 4 node groups; expert e belongs to node group e // 2. slots[t, n] is below 8 exactly where some expert of token t belongs to node group n, and equals 8 elsewhere; within each aligned block of 8 rows (the rows of one device) the values below 8 in one column are distinct.
All inputs are finite; a program needn't handle non-finite values.
Results may differ from a plain program's by a relative error of at most 0.019.
Values may be sent and summed in bfloat16 or wider, within the bound.
A program may use at most 192 MiB of HBM per device.

v0:
```python
import jax
import jax.numpy as jnp
from jax import lax
from jax.sharding import PartitionSpec as P


def expert_terms(row_block, row_gates, w_gate, w_up, w_down):
    summed = jnp.zeros((row_block.shape[0], w_down.shape[2]), jnp.float32)
    for member in range(w_gate.shape[0]):
        gate_value = jnp.dot(row_block, w_gate[member], preferred_element_type=jnp.float32)
        up_value = jnp.dot(row_block, w_up[member], preferred_element_type=jnp.float32)
        hidden = (jax.nn.silu(gate_value) * up_value).astype(jnp.bfloat16)
        output = jnp.dot(hidden, w_down[member], preferred_element_type=jnp.float32)
        summed = summed + row_gates[:, member : member + 1].astype(jnp.float32) * output
    return summed


def local(tokens, expert_ids, gate_weights, slots, w_gate, w_up, w_down):
    node_count = lax.axis_size("node")
    token_count = tokens.shape[0]
    model_width = tokens.shape[1]
    per_node = w_gate.shape[0]
    experts_all = node_count * per_node
    matches = (
        expert_ids[:, :, None] == jnp.arange(experts_all, dtype=jnp.int32)[None, None, :]
    ).astype(jnp.float32)
    token_gates = jnp.sum(gate_weights.astype(jnp.float32)[:, :, None] * matches, axis=1)
    token_gates = token_gates.reshape(token_count, node_count, per_node)
    picked = slots.T[:, None, :] == jnp.arange(token_count, dtype=jnp.int32)[None, :, None]
    send_rows = jnp.einsum(
        "nct,td->ncd", picked.astype(jnp.bfloat16), tokens, preferred_element_type=jnp.float32
    ).astype(jnp.bfloat16)
    send_gates = jnp.einsum(
        "nct,tne->nce", picked.astype(jnp.float32), token_gates, precision=lax.Precision.HIGHEST
    ).astype(jnp.bfloat16)
    got_rows, got_gates = (
        lax.all_to_all(send_rows, "node", split_axis=0, concat_axis=0, tiled=True),
        lax.all_to_all(send_gates, "node", split_axis=0, concat_axis=0, tiled=True),
    )
    piece_rows, piece_gates = lax.all_gather(
        (got_rows[:, None], got_gates[:, None]), "local", axis=1, tiled=True
    )
    row_shape = piece_rows.shape
    row_terms = expert_terms(
        piece_rows.reshape(-1, model_width), piece_gates.reshape(-1, per_node), w_gate, w_up, w_down
    )
    partial_value = row_terms.reshape(row_shape)
    node_sums = lax.psum_scatter(
        partial_value.astype(jnp.bfloat16), "local", scatter_dimension=1, tiled=True
    ).astype(jnp.float32)
    back_rows = node_sums.reshape(node_count, token_count, model_width).astype(jnp.bfloat16)
    returned = lax.all_to_all(back_rows, "node", split_axis=0, concat_axis=0, tiled=True)
    combined = jnp.einsum(
        "nct,ncd->td", picked.astype(jnp.bfloat16), returned, preferred_element_type=jnp.float32
    )
    return combined.astype(jnp.bfloat16)


def solution(mesh):
    in_specs = (
        P(("parts", "node", "local"), None),
        P(("parts", "node", "local"), None),
        P(("parts", "node", "local"), None),
        P(("parts", "node", "local"), None),
        P(("parts", "node"), None, "local"),
        P(("parts", "node"), None, "local"),
        P(("parts", "node"), "local", None),
    )
    out_specs = P(("parts", "node", "local"), None)
    return jax.shard_map(local, mesh=mesh, in_specs=in_specs, out_specs=out_specs, check_vma=False)
```

profile of v0, /device:TPU:0, one launch (start us, length us, event | category | flops | bytes accessed | tf_op | source)
XLA Modules:
  0.0 132.3 jit_solution(16588762243438808216)
XLA Ops:
  6.5 0.0 copy-start
  6.5 0.0 all-gather.4.cloned.1.call-start
  6.5 0.9 copy-done
  7.4 1.1 convolution_convert_fusion
  8.5 19.3 %all_to_all.15 = bf16[4,8,7168]{2,1,0:T(8,128)(2,1)} all-to-all(bf16[4,8,7168]{2,1,0:T(8,128)(2,1)S(1)} %convolution_convert_fusion), channel_id=1, replica_groups=mesh['parts'=2,'node'=4,'local'=4] {'node'}, dimensions={0} | all-to-all | bytes 917504 | tf_op jit(solution)/shard_map/all_to_all | solution.py:37
  27.8 0.0 all-gather.4.cloned.1.call-update
  27.9 0.0 reduce-scatter.2.cloned.1.call-start
  27.9 0.7 convert_element_type.35
  28.6 0.8 select_reduce_fusion
  29.4 0.1 copy.20
  29.5 0.9 convolution_convert_fusion.1
  30.3 8.1 %all_to_all.16 = bf16[4,8,2]{1,2,0:T(2,128)(2,1)S(1)} all-to-all(bf16[4,8,2]{1,2,0:T(2,128)(2,1)S(1)} %convolution_convert_fusion.1), channel_id=1, replica_groups=mesh['parts'=2,'node'=4,'local'=4] {'node'}, dimensions={0} | all-to-all | bytes 256 | tf_op jit(solution)/shard_map/all_to_all | solution.py:38
  38.4 0.1 copy.22
  38.5 5.4 %all-gather = bf16[4,32,2]{0,2,1:T(2,128)(2,1)S(1)} all-gather(bf16[4,8,2]{0,2,1:T(2,128)(2,1)S(1)} %copy.22), channel_id=2, replica_groups=mesh['parts'=2,'node'=4,'local'=4] {'local'}, dimensions={1}, use_global_device_ids=true | all-gather | bytes 640 | tf_op jit(solution)/shard_map/all_gather | solution.py:40
  43.9 0.1 copy.23
  44.0 0.1 reshape.17
  44.1 4.2 %all-gather.4.cloned.1.call-done = bf16[4,32,7168]{2,1,0:T(8,128)(2,1)} async-done(((bf16[4,8,7168]{2,1,0:T(8,128)(2,1)}), bf16[4,32,7168]{2,1,0:T(8,128)(2,1)}) %all-gather.4.cloned.1.call-update) | async-done | bytes 1835024 | tf_op jit(solution)/shard_map/all_gather | solution.py:40
  48.3 0.0 copy-start.2
  48.3 4.9 %fusion.6 = f32[128,512]{1,0:T(8,128)S(1)} fusion(bf16[128,7168]{1,0:T(8,128)(2,1)} %bitcast.62, bf16[2,7168,512]{2,1,0:T(8,128)(2,1)} %param.11), kind=kOutput, calls=%fused_computation.10 | convolution fusion | flops 939524096 | bytes 9437184 | tf_op jit(solution)/shard_map/dot_general | solution.py:10
  53.2 0.0 copy-done.2
  53.2 4.2 %fusion.11 = f32[128,512]{1,0:T(8,128)S(1)} fusion(bf16[128,7168]{1,0:T(8,128)(2,1)S(1)} %bitcast.64, bf16[2,7168,512]{2,1,0:T(8,128)(2,1)} %param.11), kind=kOutput, calls=%fused_computation.15 | convolution fusion | flops 939524096 | bytes 9437184 | tf_op jit(solution)/shard_map/dot_general | solution.py:10
  57.4 9.2 %convolution_multiply_fusion.1 = f32[128,7168]{1,0:T(8,128)} fusion(bf16[2,512,7168]{2,1,0:T(8,128)(2,1)} %param.13, f32[128]{0:T(128)S(1)} %get-tuple-element.6, bf16[128,7168]{1,0:T(8,128)(2,1)S(1)} %bitcast.65, bf16[2,7168,512]{2,1,0:T(8,128)(2,1)} %param.12, f32[128,512]{1,0:T(8,128)S(1)} %fusion.11), kind=kOutput, calls=%fused_computation.2 | convolution fusion | flops 1880358912 | bytes 20447744 | tf_op jit(solution)/shard_map/dot_general | solution.py:13
  66.6 0.0 copy-start.1
  66.6 9.0 %fusion.1 = bf16[128,7168]{1,0:T(8,128)(2,1)S(1)} fusion(f32[128,7168]{1,0:T(8,128)} %convolution_multiply_fusion.1, bf16[2,512,7168]{2,1,0:T(8,128)(2,1)} %param.13, f32[128]{0:T(128)S(1)} %get-tuple-element.5, bf16[128,7168]{1,0:T(8,128)(2,1)} %bitcast.63, bf16[2,7168,512]{2,1,0:T(8,128)(2,1)} %param.12, f32[128,512]{1,0:T(8,128)S(1)} %fusion.6), kind=kOutput, calls=%fused_computation.3 | convolution fusion | flops 1882193920 | bytes 22282752 | tf_op jit(solution)/shard_map/dot_general | solution.py:13
  75.6 1.4 %copy.25 = bf16[4,4,8,7168]{3,2,0,1:T(8,128)(2,1)} copy(bf16[4,4,8,7168]{3,2,1,0:T(8,128)(2,1)S(1)} %bitcast.56) | data formatting | bytes 3670016 | tf_op jit(solution)/shard_map/convert_element_type | solution.py:49
  77.0 0.0 reduce-scatter.2.cloned.1.call-update
  77.0 29.8 %reduce-scatter.2.cloned.1.call-done = bf16[4,1,8,7168]{3,2,0,1:T(8,128)(2,1)} async-done(((bf16[4,4,8,7168]{3,2,0,1:T(8,128)(2,1)}), bf16[4,1,8,7168]{3,2,0,1:T(8,128)(2,1)}) %reduce-scatter.2.cloned.1.call-update) | async-done | bytes 458768 | tf_op jit(solution)/shard_map/reduce_scatter | solution.py:48
  106.8 17.5 %all_to_all.17 = bf16[4,8,7168]{2,1,0:T(8,128)(2,1)S(1)} all-to-all(bf16[4,8,7168]{2,1,0:T(8,128)(2,1)} %bitcast.57), channel_id=1, replica_groups=mesh['parts'=2,'node'=4,'local'=4] {'node'}, dimensions={0} | all-to-all | bytes 917504 | tf_op jit(solution)/shard_map/all_to_all | solution.py:52
  124.3 0.0 copy-done.1
  124.3 1.1 fusion.2
  (1 shorter events, 0.0 us)
Async XLA Ops:
  6.5 0.9 copy-start
  6.5 41.8 %all-gather.4.cloned.1.call-start = ((), (), s32[]{:S(2)}) async-start(), calls=%async_computation.5 | async-start | bytes 2293760 | tf_op jit(solution)/shard_map/all_gather | solution.py:40
  27.9 78.9 %reduce-scatter.2.cloned.1.call-start = ((), (), s32[]{:S(2)}) async-start(), calls=%async_computation.4 | async-start | bytes 2293760 | tf_op jit(solution)/shard_map/reduce_scatter | solution.py:48
  48.3 4.9 %copy-start.2 = (bf16[4,32,7168]{2,1,0:T(8,128)(2,1)S(1)}, bf16[4,32,7168]{2,1,0:T(8,128)(2,1)}, u32[]{:S(2)}) copy-start(bf16[4,32,7168]{2,1,0:T(8,128)(2,1)} %all-gather.4.cloned.1.call-done) | copy-start | bytes 5505028
  66.6 57.7 %copy-start.1 = (s32[8,4]{0,1:T(4,128)S(1)}, s32[8,4]{0,1:T(4,128)}, u32[]{:S(2)}) copy-start(s32[8,4]{0,1:T(4,128)} %param.10) | copy-start | bytes 388
Sparse Core Ops, SparseCore 0:
  28.0 20.2 all-gather.3
  77.2 29.6 reduce-scatter.1
where the time goes:
time: 133 us; the launch traced here: 132 us
  blocking collectives  50.3 us (38%)
  waiting for transfers between devices  34 us (26%)
  matrix products  30.4 us (23%)
  between operations  13.5 us (10%)
  local copies, waits for them, and re-layouts  2.64 us (2%)
  other arithmetic  1.47 us (1%)
    reduce_scatter x1, waiting for transfers between devices, local(): lax.psum_scatter(partial_value.astype(jnp.bfloat16), 'local', scatter_dim...  29.8 us
    all_to_all x1, blocking collectives, local(): lax.all_to_all(send_rows, 'node', split_axis=0, concat_axis=0, tiled=True)  19.3 us
    dot_general x2, matrix products, expert_terms(): output = jnp.dot(hidden, w_down[member], preferred_element_type=jnp.float32)  18.2 us
    all_to_all x1, blocking collectives, local(): lax.all_to_all(back_rows, 'node', split_axis=0, concat_axis=0, tiled=True)  17.5 us
    dot_general x2, matrix products, expert_terms(): jnp.dot(row_block, w_gate[member], preferred_element_type=jnp.float32)  9.08 us
    all_to_all x1, blocking collectives, local(): lax.all_to_all(send_gates, 'node', split_axis=0, concat_axis=0, tiled=True)  8.11 us
    all_gather x1, blocking collectives, local(): lax.all_gather((got_rows[:, None], got_gates[:, None]), 'local', axis=1,...  5.38 us
    all_gather x1, waiting for transfers between devices, local(): lax.all_gather((got_rows[:, None], got_gates[:, None]), 'local', axis=1,...  4.19 us
  transfers between devices with their start and end apart: 2, of which 2 were waited for; matrix products, arithmetic and copies ran while one was open for 2% of the time, Pallas kernels for 0%

commit v1 on v0

v1 whole, which is shorter than its diff:
```python
import functools

import jax
import jax.numpy as jnp
from jax import lax
from jax.experimental import pallas as pl
from jax.experimental.pallas import tpu as pltpu
from jax.sharding import PartitionSpec as P

MESH = pl.DeviceIdType.MESH
LANES = 128


def split_count(width):
    for count in (7, 8, 4, 2):
        if width % (count * LANES) == 0:
            return count
    return 1


def loop(count, body):
    if count == 1:
        body(0)
    else:
        lax.fori_loop(0, count, lambda i, c: (body(i), c)[1], 0)


def kernel(N, Q, T, K, KR,
           tokens, ids, gw, slots, wg, wu, wd, out,
           X, PO, RC, RY, S2, RZ, WG, WU, WD, acc, hid, ids_v, gw_v, sl_v,
           sm, sw, sd, az_s, az_r, ay_s, ay_r, ac_s, ac_r,
           rc_s, rc_r, ry_s, ry_r, rz_s, rz_r):
    D = tokens.shape[1]
    E, _, F = wg.shape
    n = lax.axis_index("node")
    l = lax.axis_index("local")
    q, c = l // 2, lax.rem(l, 2)
    kc, nc = D // K, D // KR
    blocks = 2 * Q * N
    rows = 128 if (blocks * T) % 128 == 0 else blocks * T
    rblk = rows // T
    rcount = blocks // rblk

    def col(k):
        return pl.ds(k * kc, kc + (LANES if k == K - 1 else 0))

    def ocol(k):
        return pl.ds(k * nc, nc)

    def blk(cc, qq, nn):
        return (cc * Q + qq) * N + nn

    def to_node(d):
        return {"node": lax.rem(n + d, N)}

    def to_y(d):
        return {"local": lax.rem(q + d, Q) * 2 + c}

    to_core = {"local": q * 2 + 1 - c}

    def remote(src, dst, ss, rs, dev):
        return pltpu.make_async_remote_copy(
            src_ref=src, dst_ref=dst, send_sem=ss, recv_sem=rs,
            device_id=dev, device_id_type=MESH)

    me = blk(c, q, n)
    small = [
        pltpu.make_async_copy(tokens, X.at[me, :, pl.ds(0, D)], sm.at[0]),
        pltpu.make_async_copy(ids, ids_v, sm.at[1]),
        pltpu.make_async_copy(gw, gw_v, sm.at[2]),
        pltpu.make_async_copy(slots, sl_v, sm.at[3]),
    ]
    for cp in small:
        cp.start()
    wcp = []
    for k in range(K):
        rs = pl.ds(k * kc, kc)
        pair = [pltpu.make_async_copy(wg.at[:, rs, :], WG.at[:, rs, :], sw.at[k, 0]),
                pltpu.make_async_copy(wu.at[:, rs, :], WU.at[:, rs, :], sw.at[k, 1])]
        wcp.append(pair)
        for cp in pair:
            cp.start()
    dcp = []
    for k in range(KR):
        cp = pltpu.make_async_copy(wd.at[:, :, ocol(k)], WD.at[:, :, ocol(k)], sd.at[k])
        cp.start()
        dcp.append(cp)

    barrier = pltpu.get_barrier_semaphore()
    for d in range(1, N):
        pl.semaphore_signal(barrier, inc=1, device_id=to_node(d), device_id_type=MESH)
    for d in range(1, Q):
        pl.semaphore_signal(barrier, inc=1, device_id=to_y(d), device_id_type=MESH)
    pl.semaphore_signal(barrier, inc=1, device_id=to_core, device_id_type=MESH)

    for cp in small:
        cp.wait()
    lane = lax.broadcasted_iota(jnp.int32, (T, LANES), 1)
    gates = jnp.zeros((T, LANES), jnp.float32)
    idv, gwv, slv = ids_v[...], gw_v[...].astype(jnp.float32), sl_v[...]
    for t in range(idv.shape[1]):
        gates = gates + jnp.where(idv[:, t:t + 1] == lane, gwv[:, t:t + 1], 0.0)
    reached = jnp.zeros((T, LANES), jnp.float32)
    for g in range(N):
        mine = (lane >= g * E) & (lane < (g + 1) * E)
        reached = reached + jnp.where(mine & (slv[:, g:g + 1] < T), 1.0, 0.0)
    X[me, :, pl.ds(D, LANES)] = (gates * reached).astype(X.dtype)
    pl.semaphore_wait(barrier, N - 1 + Q - 1 + 1)

    pending = []

    def send(src, dst, ss, rs, dev):
        cp = remote(src, dst, ss, rs, dev)
        cp.start()
        pending.append(cp)

    def z_copy(k, d):
        b = X.at[me, :, col(k)]
        return b, b, az_s.at[k, d - 1], az_r.at[k, d - 1], to_node(d)

    def y_copy(k, dq, d):
        b = X.at[blk(c, q, lax.rem(n - d + N, N)), :, col(k)]
        return b, b, ay_s.at[k, dq - 1, d], ay_r.at[k, dq - 1, d], to_y(dq)

    def c_copy(k, dq):
        b = X.at[pl.ds(blk(c, lax.rem(q - dq + Q, Q), 0), N), :, col(k)]
        return b, b, ac_s.at[k, dq], ac_r.at[k, dq], to_core

    for k in range(K):
        for d in range(1, N):
            send(*z_copy(k, d))
        for dq in range(1, Q):
            send(*y_copy(k, dq, 0))

    def z_forward(k):
        for d in range(1, N):
            remote(*z_copy(k, d)).wait_recv()
            for dq in range(1, Q):
                send(*y_copy(k, dq, d))
        send(*c_copy(k, 0))

    def y_forward(k):
        for dq in range(1, Q):
            for d in range(N):
                remote(*y_copy(k, dq, d)).wait_recv()
            send(*c_copy(k, dq))

    def project(k):
        for dq in range(Q):
            remote(*c_copy(k, dq)).wait_recv()
        for cp in wcp[k]:
            cp.wait()

        def row_body(r):
            rb = pl.ds(r * rblk, rblk)
            ro = pl.ds(r * rows, rows)
            x = X[rb, :, pl.ds(k * kc, kc)].astype(jnp.float32)
            x = x.reshape(rows, kc).astype(jnp.bfloat16)

            def member(e):
                for i, W in enumerate((WG, WU)):
                    part = jnp.dot(x, W[e, pl.ds(k * kc, kc), :],
                                   preferred_element_type=jnp.float32)
                    if k == 0:
                        acc[i, e, ro, :] = part
                    else:
                        acc[i, e, ro, :] = acc[i, e, ro, :] + part

            loop(E, member)

        loop(rcount, row_body)

    for s in range(K + 2):
        if s < K:
            z_forward(s)
        if 1 <= s <= K:
            y_forward(s - 1)
        if s >= 2:
            project(s - 2)

    def hidden_body(r):
        rb = pl.ds(r * rblk, rblk)
        ro = pl.ds(r * rows, rows)
        g = X[rb, :, pl.ds(D, LANES)].astype(jnp.float32).reshape(rows, LANES)
        lanes = lax.broadcasted_iota(jnp.int32, (rows, LANES), 1)
        for e in range(E):
            w = jnp.sum(jnp.where(lanes == n * E + e, g, 0.0), axis=1, keepdims=True)
            v, u = acc[0, e, ro, :], acc[1, e, ro, :]
            h = v / (1.0 + jnp.exp(-v)) * u * w
            hid[ro, pl.ds(e * F, F)] = h.astype(hid.dtype)

    loop(rcount, hidden_body)

    half = Q * N
    step = 512 if nc % 512 == 0 else nc

    def rc_copy(k):
        return (PO.at[pl.ds((1 - c) * half, half), :, ocol(k)], RC.at[:, :, ocol(k)],
                rc_s.at[k], rc_r.at[k], to_core)

    def ry_copy(k, dq):
        return (PO.at[pl.ds(blk(c, lax.rem(q + dq, Q), 0), N), :, ocol(k)],
                RY.at[dq - 1, :, :, ocol(k)], ry_s.at[k, dq - 1], ry_r.at[k, dq - 1], to_y(dq))

    def rz_copy(k, d):
        return (S2.at[lax.rem(n + d, N), :, ocol(k)], RZ.at[d - 1, :, ocol(k)],
                rz_s.at[k, d - 1], rz_r.at[k, d - 1], to_node(d))

    def down(k):
        dcp[k].wait()

        def row_body(r):
            rb = pl.ds(r * rblk, rblk)
            h = hid[pl.ds(r * rows, rows), :]

            def col_body(j):
                cs = pl.ds(pl.multiple_of(k * nc + j * step, LANES), step)
                w = WD[:, :, cs].reshape(E * F, step)
                o = jnp.dot(h, w, preferred_element_type=jnp.float32)
                PO[rb, :, cs] = o.reshape(rblk, T, step).astype(PO.dtype)

            loop(nc // step, col_body)

        loop(rcount, row_body)
        send(*rc_copy(k))

    def core_sum(k):
        remote(*rc_copy(k)).wait_recv()
        mine = pl.ds(c * half, half)
        PO[mine, :, ocol(k)] = (PO[mine, :, ocol(k)].astype(jnp.float32)
                                + RC[:, :, ocol(k)].astype(jnp.float32)).astype(PO.dtype)
        for dq in range(1, Q):
            send(*ry_copy(k, dq))

    def y_sum(k):
        total = PO[pl.ds(blk(c, q, 0), N), :, ocol(k)].astype(jnp.float32)
        for dq in range(1, Q):
            remote(*ry_copy(k, dq)).wait_recv()
            total = total + RY[dq - 1, :, :, ocol(k)].astype(jnp.float32)
        S2[:, :, ocol(k)] = total.astype(S2.dtype)
        for d in range(1, N):
            send(*rz_copy(k, d))

    def z_sum(k):
        total = S2[n, :, ocol(k)].astype(jnp.float32)
        for d in range(1, N):
            remote(*rz_copy(k, d)).wait_recv()
            total = total + RZ[d - 1, :, ocol(k)].astype(jnp.float32)
        out[:, ocol(k)] = total.astype(out.dtype)

    for s in range(KR + 3):
        if s < KR:
            down(s)
        if 1 <= s <= KR:
            core_sum(s - 1)
        if 2 <= s <= KR + 1:
            y_sum(s - 2)
        if s >= 3:
            z_sum(s - 3)

    for cp in pending:
        cp.wait_send()


def local(N, L, tokens, ids, gw, slots, wg, wu, wd):
    Q = L // 2
    T, D = tokens.shape
    E, _, F = wg.shape
    K = KR = split_count(D)
    blocks = N * L
    bf, f32 = jnp.bfloat16, jnp.float32
    dma = pltpu.SemaphoreType.DMA
    anyspec = pl.BlockSpec(memory_space=pl.ANY)
    return pl.pallas_call(
        functools.partial(kernel, N, Q, T, K, KR),
        out_shape=jax.ShapeDtypeStruct((T, D), bf),
        in_specs=[anyspec] * 7,
        out_specs=pl.BlockSpec(memory_space=pltpu.VMEM),
        scratch_shapes=[
            pltpu.VMEM((blocks, T, D + LANES), bf),
            pltpu.VMEM((blocks, T, D), bf),
            pltpu.VMEM((Q * N, T, D), bf),
            pltpu.VMEM((Q - 1, N, T, D), bf),
            pltpu.VMEM((N, T, D), bf),
            pltpu.VMEM((N - 1, T, D), bf),
            pltpu.VMEM((E, D, F), bf),
            pltpu.VMEM((E, D, F), bf),
            pltpu.VMEM((E, F, D), bf),
            pltpu.VMEM((2, E, blocks * T, F), f32),
            pltpu.VMEM((blocks * T, E * F), bf),
            pltpu.VMEM(ids.shape, ids.dtype),
            pltpu.VMEM(gw.shape, gw.dtype),
            pltpu.VMEM(slots.shape, slots.dtype),
            dma((4,)), dma((K, 2)), dma((KR,)),
            dma((K, N - 1)), dma((K, N - 1)),
            dma((K, Q - 1, N)), dma((K, Q - 1, N)),
            dma((K, Q)), dma((K, Q)),
            dma((KR,)), dma((KR,)),
            dma((KR, Q - 1)), dma((KR, Q - 1)),
            dma((KR, N - 1)), dma((KR, N - 1)),
        ],
        compiler_params=pltpu.CompilerParams(
            collective_id=0, has_side_effects=True, vmem_limit_bytes=67043328),
    )(tokens, ids, gw, slots, wg, wu, wd)


def solution(mesh):
    N, L = mesh.shape["node"], mesh.shape["local"]
    rows = P(("parts", "node", "local"), None)
    up = P(("parts", "node"), None, "local")
    return jax.shard_map(
        functools.partial(local, N, L), mesh=mesh,
        in_specs=(rows, rows, rows, rows, up, up, P(("parts", "node"), "local", None)),
        out_specs=rows, check_vma=False)
```

time: 133 us -> 66.8 us (0.50)
  Pallas kernels: 0 us -> 63.7 us
  blocking collectives: 50.3 us -> 0 us
  waiting for transfers between devices: 34 us -> 0 us
  matrix products: 30.4 us -> 0 us
  between operations: 13.5 us -> 0.01 us
  other arithmetic: 1.47 us -> 0 us
    pallas_call x0 -> x1, Pallas kernels: none -> 63.7 us  [local(): pl.pallas_call(functools.partial(kernel, N, Q, T, K, KR), out_shape=jax.S...]
    all_to_all x3 -> x0, blocking collectives: 44.9 us -> none  [the longest x1 19.3 us: local(): lax.all_to_all(send_rows, 'node', split_axis=0, concat_axis=0, tiled=True)]
    dot_general x7 -> x0, matrix products: 30.4 us -> none  [the longest x2 18.2 us: expert_terms(): output = jnp.dot(hidden, w_down[member], preferred_element_type=jnp.float32)]
    reduce_scatter x1 -> x0, waiting for transfers between devices: 29.8 us -> none  [local(): lax.psum_scatter(partial_value.astype(jnp.bfloat16), 'local', scatter_dim...]
    all_gather x1 -> x0, blocking collectives: 5.38 us -> none  [local(): lax.all_gather((got_rows[:, None], got_gates[:, None]), 'local', axis=1,...]
    all_gather x1 -> x0, waiting for transfers between devices: 4.19 us -> none  [local(): lax.all_gather((got_rows[:, None], got_gates[:, None]), 'local', axis=1,...]
    unnamed x6 -> x2, local copies, waits for them, and re-layouts: 0.9 us -> 2.9 us
    convert_element_type x1 -> x0, local copies, waits for them, and re-layouts: 1.38 us -> none  [local(): partial_value.astype(jnp.bfloat16)]
  transfers between devices with their start and end apart: 2 -> 0, of which waited for: 2 -> 0; matrix products, arithmetic and copies ran while one was open for 2% -> 0% of each run, Pallas kernels for 0% -> 0%
where the time goes in v1:
time: 66.8 us; the launch traced here: 66.6 us
  Pallas kernels  63.7 us (95%)
  local copies, waits for them, and re-layouts  2.9 us (4%)
    pallas_call x1, Pallas kernels, local(): pl.pallas_call(functools.partial(kernel, N, Q, T, K, KR), out_shape=jax.S...  63.7 us
    unnamed x2, local copies, waits for them, and re-layouts  2.9 us

profile of v1, /device:TPU:0, one launch (start us, length us, event | category | flops | bytes accessed | tf_op | source)
XLA Modules:
  0.0 66.6 jit_solution(6681343556134613440)
XLA Ops:
  0.0 1.3 %copy.8.slots = s32[8,4]{1,0:T(8,128)} copy(s32[8,4]{0,1:T(4,128)} %param.10) | data formatting | bytes 256 | tf_op args[3]
  1.3 63.7 %shard_map.73 = bf16[8,7168]{1,0:T(8,128)(2,1)} custom-call(bf16[8,7168]{1,0:T(8,128)(2,1)} %tokens.1, s32[8,8]{1,0:T(8,128)} %ids.1, bf16[8,8]{1,0:T(8,128)(2,1)} %gw.1, s32[8,4]{1,0:T(8,128)} %copy.8.slots, bf16[2,7168,512]{2,1,0:T(8,128)(2,1)} %wg.1, bf16[2,7168,512]{2,1,0:T(8,128)(2,1)} %wu.1, bf16[2,512,7168]{2,1,0:T(8,128)(2,1)} %wd.1), custom_call_target="tpu_custom_call" | custom-call | tf_op jit(solution)/shard_map/pallas_call | solution.py:274
  65.1 1.6 %copy.10 = bf16[8,7168]{1,0:T(8,128)(2,1)} copy(bf16[8,7168]{1,0:T(8,128)(2,1)} %shard_map.73) | data formatting | bytes 229376

commit v2 on v1

--- a/solution.py
+++ b/solution.py
@@ -12,7 +12,7 @@
 
 
 def split_count(width):
-    for count in (7, 8, 4, 2):
+    for count in (4, 7, 2):
         if width % (count * LANES) == 0:
             return count
     return 1
@@ -79,11 +79,11 @@
                 pltpu.make_async_copy(wu.at[:, rs, :], WU.at[:, rs, :], sw.at[k, 1])]
         wcp.append(pair)
         for cp in pair:
-            cp.start()
+            cp.start(priority=1)
     dcp = []
     for k in range(KR):
         cp = pltpu.make_async_copy(wd.at[:, :, ocol(k)], WD.at[:, :, ocol(k)], sd.at[k])
-        cp.start()
+        cp.start(priority=1)
         dcp.append(cp)
 
     barrier = pltpu.get_barrier_semaphore()
@@ -97,13 +97,15 @@
         cp.wait()
     lane = lax.broadcasted_iota(jnp.int32, (T, LANES), 1)
     gates = jnp.zeros((T, LANES), jnp.float32)
-    idv, gwv, slv = ids_v[...], gw_v[...].astype(jnp.float32), sl_v[...]
+    idv, gwv, slv = ids_v[...], gw_v[...].astype(jnp.float32), sl_v[...].astype(jnp.float32)
     for t in range(idv.shape[1]):
         gates = gates + jnp.where(idv[:, t:t + 1] == lane, gwv[:, t:t + 1], 0.0)
     reached = jnp.zeros((T, LANES), jnp.float32)
+    eye = lax.broadcasted_iota(jnp.int32, (T, T), 0) == lax.broadcasted_iota(jnp.int32, (T, T), 1)
     for g in range(N):
+        slot = jnp.sum(jnp.where(eye, slv[g:g + 1, :], 0.0), axis=1, keepdims=True)
         mine = (lane >= g * E) & (lane < (g + 1) * E)
-        reached = reached + jnp.where(mine & (slv[:, g:g + 1] < T), 1.0, 0.0)
+        reached = reached + jnp.where(mine & (slot < T), 1.0, 0.0)
     X[me, :, pl.ds(D, LANES)] = (gates * reached).astype(X.dtype)
     pl.semaphore_wait(barrier, N - 1 + Q - 1 + 1)
 
@@ -192,7 +194,7 @@
     loop(rcount, hidden_body)
 
     half = Q * N
-    step = 512 if nc % 512 == 0 else nc
+    step = nc // 2 if nc % (2 * LANES) == 0 else nc
 
     def rc_copy(k):
         return (PO.at[pl.ds((1 - c) * half, half), :, ocol(k)], RC.at[:, :, ocol(k)],
@@ -290,7 +292,7 @@
             pltpu.VMEM((blocks * T, E * F), bf),
             pltpu.VMEM(ids.shape, ids.dtype),
             pltpu.VMEM(gw.shape, gw.dtype),
-            pltpu.VMEM(slots.shape, slots.dtype),
+            pltpu.VMEM(slots.shape[::-1], slots.dtype),
             dma((4,)), dma((K, 2)), dma((KR,)),
             dma((K, N - 1)), dma((K, N - 1)),
             dma((K, Q - 1, N)), dma((K, Q - 1, N)),
@@ -301,7 +303,7 @@
         ],
         compiler_params=pltpu.CompilerParams(
             collective_id=0, has_side_effects=True, vmem_limit_bytes=67043328),
-    )(tokens, ids, gw, slots, wg, wu, wd)
+    )(tokens, ids, gw, slots.T, wg, wu, wd)
 
 
 def solution(mesh):

time: 66.8 us -> 48 us (0.72)
  Pallas kernels: 63.7 us -> 46.3 us
  local copies, waits for them, and re-layouts: 2.9 us -> 1.55 us
    pallas_call x1, Pallas kernels: 63.7 us -> 46.3 us  [local(): pl.pallas_call(functools.partial(kernel, N, Q, T, K, KR), out_shape=jax.S...]
    unnamed x2 -> x1, local copies, waits for them, and re-layouts: 2.9 us -> 1.55 us
where the time goes in v2:
time: 48 us; the launch traced here: 47.9 us
  Pallas kernels  46.3 us (96%)
  local copies, waits for them, and re-layouts  1.55 us (3%)
    pallas_call x1, Pallas kernels, local(): pl.pallas_call(functools.partial(kernel, N, Q, T, K, KR), out_shape=jax.S...  46.3 us
    unnamed x1, local copies, waits for them, and re-layouts  1.55 us

profile of v2, /device:TPU:0, one launch (start us, length us, event | category | flops | bytes accessed | tf_op | source)
XLA Modules:
  0.0 47.9 jit_solution(15960180912860025311)
XLA Ops:
  0.0 46.3 %shard_map.73 = bf16[8,7168]{1,0:T(8,128)(2,1)} custom-call(bf16[8,7168]{1,0:T(8,128)(2,1)} %tokens.1, s32[8,8]{1,0:T(8,128)} %ids.1, bf16[8,8]{1,0:T(8,128)(2,1)} %gw.1, s32[4,8]{1,0:T(4,128)} %bitcast.1, bf16[2,7168,512]{2,1,0:T(8,128)(2,1)} %wg.1, bf16[2,7168,512]{2,1,0:T(8,128)(2,1)} %wu.1, bf16[2,512,7168]{2,1,0:T(8,128)(2,1)} %wd.1), custom_call_target="tpu_custom_call" | custom-call | tf_op jit(solution)/shard_map/pallas_call | solution.py:276
  46.3 1.6 %copy.9 = bf16[8,7168]{1,0:T(8,128)(2,1)} copy(bf16[8,7168]{1,0:T(8,128)(2,1)} %shard_map.73) | data formatting | bytes 229376
